TPU v7x, 512 devices: a whole 4x4x16 slice. The times are simulated.
512 devices in a mesh: dp: 32 (over x, y, core), expert: 16 (over z).
Axes of the slice: x: 4, y: 4, z: 16, core: 2. Of those that a mesh axis runs over, the one named last changes fastest.
Arguments:
- tokens: bfloat16 [4096, 2048], P('dp', 'expert'), may hold values from -6 to 6
- cotangent: bfloat16 [4096, 2048], P('dp', 'expert'), may hold values from -6 to 6
- expert_ids: int32 [4096, 8], P('dp'), may hold values from 0 to 127, all different within a row; in each aligned block of 128 rows (0 to 127, 128 to 255, ...) at most 16 rows name the same one
- gate_weights: float32 [4096, 8], P('dp'), may hold values from 0.05 to 1
- w_gate: bfloat16 [512, 192, 2048], P(('dp', 'expert')), may hold values from -0.125 to 0.125
- w_up: bfloat16 [512, 192, 2048], P(('dp', 'expert')), may hold values from -0.125 to 0.125
- w_down: bfloat16 [512, 192, 2048], P(('dp', 'expert')), may hold values from -0.21875 to 0.21875
Outputs:
- layer_out: bfloat16 [4096, 2048], P('dp', 'expert')
- grad_tokens: bfloat16 [4096, 2048], P('dp', 'expert')
- grad_gates: float32 [4096, 8], P('dp')
- grad_w_gate: bfloat16 [512, 192, 2048], P(('dp', 'expert'))
- grad_w_up: bfloat16 [512, 192, 2048], P(('dp', 'expert'))
- grad_w_down: bfloat16 [512, 192, 2048], P(('dp', 'expert'))
Inputs may be any that keep to these rules, and one draw needn't show every extreme that they name: `expert_ids`: each row names 8 different experts. In each aligned block of 128 rows (the rows of one index of dp) no expert is named by more than 16 rows, and in some block an expert is named by exactly 16 rows.
All inputs are finite; a program needn't handle non-finite values.
Results may differ from a plain program's by a relative error of at most 0.0064.
Values may be sent and summed in bfloat16 or wider, within the bound.
No kernel may reach another device: no remote copies, remote signals or barrier semaphores. Data moves between devices by JAX's collectives and lax.ppermute only.
A program may use at most 64 MiB of HBM per device.

v0:
```python
import jax
import jax.numpy as jnp
from jax import lax
from jax.sharding import PartitionSpec as P

SHARDS = 4


def silu_parts(preact):
    sigmoid_of = jax.nn.sigmoid(preact)
    activated = preact * sigmoid_of
    derivative = sigmoid_of * (1.0 + preact * (1.0 - sigmoid_of))
    return (activated, derivative)


def contract_last(first_op, second_op):
    return lax.dot_general(
        first_op, second_op, (((1,), (1,)), ((), ())), preferred_element_type=jnp.float32
    )


def contract_first(first_op, second_op):
    return lax.dot_general(
        first_op, second_op, (((0,), (0,)), ((), ())), preferred_element_type=jnp.float32
    )


def forward_rows(rows_x, gate_w, up_w, down_w):
    pre_gate = contract_last(rows_x, gate_w)
    pre_up = contract_last(rows_x, up_w)
    activated, derivative = silu_parts(pre_gate)
    hidden = (activated * pre_up).astype(jnp.bfloat16)
    return jnp.dot(hidden, down_w, preferred_element_type=jnp.float32).astype(jnp.bfloat16)


def backward_rows(rows_x, rows_do, gate_w, up_w, down_w):
    pre_gate = contract_last(rows_x, gate_w)
    pre_up = contract_last(rows_x, up_w)
    activated, derivative = silu_parts(pre_gate)
    hidden = (activated * pre_up).astype(jnp.bfloat16)
    d_hidden = contract_last(rows_do, down_w)
    d_pre_gate = (d_hidden * pre_up * derivative).astype(jnp.bfloat16)
    d_pre_up = (d_hidden * activated).astype(jnp.bfloat16)
    part_grad = (
        jnp.dot(d_pre_gate, gate_w, preferred_element_type=jnp.float32)
        + jnp.dot(d_pre_up, up_w, preferred_element_type=jnp.float32)
    ).astype(jnp.bfloat16)
    gradients = (
        contract_first(d_pre_gate, rows_x),
        contract_first(d_pre_up, rows_x),
        contract_first(hidden, rows_do),
    )
    return (part_grad, gradients)


def per_device(tokens, cotangent, expert_ids, gate_weights, w_gate, w_up, w_down):
    full_x, full_dy = (
        lax.all_gather(tokens, "expert", axis=1, tiled=True),
        lax.all_gather(cotangent, "expert", axis=1, tiled=True),
    )
    dp_count = lax.axis_size("dp")
    column_count = lax.axis_size("expert")
    column = lax.axis_index("expert")
    tok_count, chosen = expert_ids.shape
    features = full_x.shape[1]
    experts_all = dp_count * column_count // SHARDS
    capacity = min(tok_count, max(2, 2 * tok_count * chosen // experts_all))
    per_row = column_count // SHARDS
    assigned = tok_count * chosen
    flat_ids = expert_ids.reshape(-1)
    flat_gates = gate_weights.reshape(-1)
    owned_here = flat_ids % per_row == column // SHARDS
    target_row = flat_ids // per_row
    onehot = (
        (target_row[:, None] == jnp.arange(dp_count, dtype=jnp.int32)[None, :])
        & owned_here[:, None]
    ).astype(jnp.int32)
    rank_of = jnp.sum((jnp.cumsum(onehot, axis=0) - 1) * onehot, axis=1)
    target = jnp.where(owned_here, target_row * capacity + rank_of, dp_count * capacity)
    slot_src = (
        jnp.full((dp_count * capacity,), assigned, jnp.int32)
        .at[target]
        .set(jnp.arange(assigned, dtype=jnp.int32), mode="drop")
    )
    filled = slot_src < assigned
    safe_index = jnp.where(filled, slot_src, 0)
    slot_token = safe_index // chosen
    slot_gate = jnp.where(filled, flat_gates[safe_index], 0.0)
    slot_dy = full_dy[slot_token].astype(jnp.float32)
    send_x = jnp.where(filled[:, None], full_x[slot_token], jnp.zeros((), full_x.dtype)).reshape(
        dp_count, capacity, features
    )
    send_do = (
        (slot_gate[:, None] * slot_dy).astype(jnp.bfloat16).reshape(dp_count, capacity, features)
    )
    weights = (w_gate[0], w_up[0], w_down[0])
    recv_x = lax.all_to_all(send_x, "dp", split_axis=0, concat_axis=0, tiled=True)
    rows_x = recv_x.reshape(dp_count * capacity, features)
    expert_out = forward_rows(rows_x, *weights)
    back_out = lax.all_to_all(
        expert_out.reshape(dp_count, capacity, features),
        "dp",
        split_axis=0,
        concat_axis=0,
        tiled=True,
    )
    recv_do = lax.all_to_all(send_do, "dp", split_axis=0, concat_axis=0, tiled=True)
    rows_do = recv_do.reshape(dp_count * capacity, features)
    part_grad, gradients = backward_rows(rows_x, rows_do, *weights)
    back_grad = lax.all_to_all(
        part_grad.reshape(dp_count, capacity, features),
        "dp",
        split_axis=0,
        concat_axis=0,
        tiled=True,
    )
    width_now = back_out.shape[2]
    out_float = back_out.reshape(dp_count * capacity, width_now).astype(jnp.float32)
    grad_float = back_grad.reshape(dp_count * capacity, width_now).astype(jnp.float32)
    out_part = (
        jnp.zeros((tok_count, width_now), jnp.float32)
        .at[slot_token]
        .add(slot_gate[:, None] * out_float)
    )
    grad_part = jnp.zeros((tok_count, width_now), jnp.float32).at[slot_token].add(grad_float)
    gate_terms = jnp.sum(slot_dy * out_float, axis=1)
    gate_part = (
        jnp.zeros((assigned,), jnp.float32)
        .at[slot_src]
        .add(gate_terms, mode="drop")
        .reshape(tok_count, chosen)
    )
    out_slice, grad_slice = (
        lax.psum_scatter(out_part, "expert", scatter_dimension=1, tiled=True),
        lax.psum_scatter(grad_part, "expert", scatter_dimension=1, tiled=True),
    )
    grad_gates = lax.psum(gate_part, "expert")
    return (
        out_slice.astype(jnp.bfloat16),
        grad_slice.astype(jnp.bfloat16),
        grad_gates,
        gradients[0].astype(jnp.bfloat16)[None],
        gradients[1].astype(jnp.bfloat16)[None],
        gradients[2].astype(jnp.bfloat16)[None],
    )


def solution(mesh):
    placed = (
        P("dp", "expert"),
        P("dp", "expert"),
        P("dp", None),
        P("dp", None),
        P(("dp", "expert"), None, None),
        P(("dp", "expert"), None, None),
        P(("dp", "expert"), None, None),
    )
    return jax.shard_map(
        per_device,
        mesh=mesh,
        in_specs=placed,
        out_specs=(
            P("dp", "expert"),
            P("dp", "expert"),
            P("dp", None),
            P(("dp", "expert"), None, None),
            P(("dp", "expert"), None, None),
            P(("dp", "expert"), None, None),
        ),
        check_vma=False,
    )
```

profile of v0, /device:TPU:2, one launch (start us, length us, event | category | flops | bytes accessed | tf_op | source)
XLA Modules:
  0.0 339.8 jit_solution(6316037226412424405)
XLA Ops:
  8.4 9.0 %reduce-window.6 = s32[32,8,128]{2,1,0:T(8,128)S(1)} reduce-window(s32[32,8,128]{2,1,0:T(8,128)S(1)} %fusion.25, s32[]{:T(128)} %constant.66.clone.1), window={size=1x1x128 pad=0_0x0_0x127_0}, to_apply=%region_0.1 | reduce-window | flops 4161536 | bytes 262148 | tf_op jit(solution)/shard_map/reduce-window
  18.0 4.3 %scatter_custom_fusion = s32[512]{0:T(512)S(1)} fusion(s32[1024]{0:T(1024)S(1)} %bitcast.72, s32[1024]{0:T(1024)S(1)} %iota.11, s32[]{:T(128)} %constant.65.clone.1), kind=kCustom, calls=%fused_computation.91 | custom fusion | bytes 2052 | tf_op jit(solution)/shard_map/scatter | solution.py:83
  22.5 38.8 %all_gather.6 = bf16[128,2048]{1,0:T(8,128)(2,1)S(1)} all-gather(bf16[128,128]{1,0:T(8,128)(2,1)} %param.7), channel_id=1, replica_groups=mesh['dp'=32,'expert'=16] {'expert'}, dimensions={1}, use_global_device_ids=true | all-gather | bytes 557056 | tf_op jit(solution)/shard_map/all_gather | solution.py:58
  65.3 7.8 %all-to-all-start = ((bf16[32,16,2048]{2,1,0:T(8,128)(2,1)}), bf16[32,16,2048]{2,1,0:T(8,128)(2,1)}, u32[]{:S(2)}, u32[]{:S(2)}) async-start(bf16[32,16,2048]{2,1,0:T(8,128)(2,1)} %broadcast_select_fusion), calls=%async_computation | async-start | bytes 4194304 | tf_op jit(solution)/shard_map/all_to_all | solution.py:97
  75.7 28.7 %all_gather.7 = bf16[128,2048]{1,0:T(8,128)(2,1)S(1)} all-gather(bf16[128,128]{1,0:T(8,128)(2,1)S(1)} %copy-done.2), channel_id=1, replica_groups=mesh['dp'=32,'expert'=16] {'expert'}, dimensions={1}, use_global_device_ids=true | all-gather | bytes 557056 | tf_op jit(solution)/shard_map/all_gather | solution.py:59
  108.6 7.4 %all-to-all-start.2 = ((bf16[32,16,2048]{2,1,0:T(8,128)(2,1)}), bf16[32,16,2048]{2,1,0:T(8,128)(2,1)}, u32[]{:S(2)}, u32[]{:S(2)}) async-start(bf16[32,16,2048]{2,1,0:T(8,128)(2,1)} %fusion), calls=%async_computation.3 | async-start | bytes 4194304 | tf_op jit(solution)/shard_map/all_to_all | solution.py:107
  116.1 3.4 %fusion.11 = f32[512,192]{0,1:T(8,128)} fusion(bf16[512,2048]{1,0:T(8,128)(2,1)} %bitcast.5, bf16[1,192,2048]{2,1,0:T(8,128)(2,1)} %param.12), kind=kOutput, calls=%fused_computation.27 | convolution fusion | flops 402653184 | bytes 3276800 | tf_op jit(solution)/shard_map/dot_general | solution.py:17
  119.5 3.2 fusion.15
  122.7 19.4 %all-to-all-done.2 = bf16[32,16,2048]{2,1,0:T(8,128)(2,1)} async-done(((bf16[32,16,2048]{2,1,0:T(8,128)(2,1)}), bf16[32,16,2048]{2,1,0:T(8,128)(2,1)}, u32[]{:S(2)}, u32[]{:S(2)}) %all-to-all-start.2) | async-done | bytes 2097184 | tf_op jit(solution)/shard_map/all_to_all | solution.py:107
  142.1 2.7 multiply_convert_fusion
  146.8 7.6 %all-to-all-start.1 = ((bf16[32,16,2048]{2,1,0:T(8,128)(2,1)}), bf16[32,16,2048]{2,1,0:T(8,128)(2,1)}, u32[]{:S(2)}, u32[]{:S(2)}) async-start(bf16[32,16,2048]{2,1,0:T(8,128)(2,1)} %bitcast.67), calls=%async_computation.1 | async-start | bytes 4194304 | tf_op jit(solution)/shard_map/all_to_all | solution.py:100
  154.7 3.8 %fusion.13 = f32[512,2048]{1,0:T(8,128)} fusion(bf16[512,192]{0,1:T(8,128)(2,1)S(1)} %get-tuple-element.15, bf16[1,192,2048]{2,1,0:T(8,128)(2,1)} %param.11), kind=kOutput, calls=%fused_computation.29 | convolution fusion | flops 402653184 | bytes 5177344 | tf_op jit(solution)/shard_map/dot_general | solution.py:45
  158.5 22.0 %all-to-all-done.1 = bf16[32,16,2048]{2,1,0:T(8,128)(2,1)} async-done(((bf16[32,16,2048]{2,1,0:T(8,128)(2,1)}), bf16[32,16,2048]{2,1,0:T(8,128)(2,1)}, u32[]{:S(2)}, u32[]{:S(2)}) %all-to-all-start.1) | async-done | bytes 2097184 | tf_op jit(solution)/shard_map/all_to_all | solution.py:100
  180.4 3.9 %bitcast_multiply_fusion = f32[512,2048]{1,0:T(8,128)} fusion(f32[512]{0:T(512)S(1)} %broadcast_select_fusion.1, bf16[32,16,2048]{2,1,0:T(8,128)(2,1)} %all-to-all-done.1), kind=kLoop, calls=%fused_computation.13 | loop fusion | flops 2097152 | bytes 6293504 | tf_op jit(solution)/shard_map/mul | solution.py:123
  184.3 9.4 %scatter_custom_fusion.1 = f32[128,2048]{1,0:T(8,128)} fusion(s32[512]{0:T(512)S(1)} %get-tuple-element.18, f32[512,2048]{1,0:T(8,128)} %bitcast_multiply_fusion, f32[]{:T(128)} %constant.64.clone.1), kind=kCustom, calls=%fused_computation.34 | custom fusion | flops 1048576 | bytes 1049088 | tf_op jit(solution)/shard_map/scatter-add | solution.py:123
  193.8 3.2 add_convert_fusion
  197.0 32.4 %all_to_all.20 = bf16[32,16,2048]{2,1,0:T(8,128)(2,1)} all-to-all(bf16[32,16,2048]{2,1,0:T(8,128)(2,1)S(1)} %bitcast.66), channel_id=1, replica_groups=mesh['dp'=32,'expert'=16] {'dp'}, dimensions={0} | all-to-all | bytes 4194304 | tf_op jit(solution)/shard_map/all_to_all | solution.py:110
  229.4 9.1 %scatter_custom_fusion.2 = f32[128,2048]{1,0:T(8,128)} fusion(s32[512]{0:T(512)S(1)} %get-tuple-element.18, bf16[512,2048]{1,0:T(8,128)(2,1)} %bitcast.68, f32[]{:T(128)} %constant.64.clone.1), kind=kCustom, calls=%fused_computation.11 | custom fusion | flops 2097152 | bytes 3145732 | tf_op jit(solution)/shard_map/scatter-add | solution.py:125
  238.6 3.1 fusion.6
  241.6 3.1 fusion.5
  244.7 3.1 fusion.4
  250.0 3.5 %scatter_custom_fusion.3 = f32[1024]{0:T(1024)S(1)} fusion(s32[512]{0:T(512)S(1)} %get-tuple-element.17, f32[512]{0:T(512)S(1)} %reshape.293, f32[]{:T(128)} %constant.64.clone.1), kind=kCustom, calls=%fused_computation.85 | custom fusion | flops 512 | bytes 4100 | tf_op jit(solution)/shard_map/scatter-add | solution.py:130
  253.6 54.9 %psum.7 = f32[128,8]{1,0:T(8,128)S(1)} all-reduce(f32[128,8]{1,0:T(8,128)S(1)} %reshape.237), channel_id=1, replica_groups=mesh['dp'=32,'expert'=16] {'expert'}, use_global_device_ids=true, to_apply=%region_10.11 | all-reduce | flops 1024 | bytes 8192 | tf_op jit(solution)/shard_map/psum | solution.py:137
  310.6 20.9 %reduce-scatter.5.cloned.1.call-done = f32[128,128]{1,0:T(8,128)} async-done(((f32[128,2048]{1,0:T(8,128)}), f32[128,128]{1,0:T(8,128)}) %reduce-scatter.5.cloned.1.call-update) | async-done | bytes 65552 | tf_op jit(solution)/shard_map/reduce_scatter | solution.py:135
  (53 shorter events, 20.9 us)
Async XLA Ops:
  7.2 134.9 %copy-start = (bf16[1,192,2048]{2,1,0:T(8,128)(2,1)S(1)}, bf16[1,192,2048]{2,1,0:T(8,128)(2,1)}, u32[]{:S(2)}) copy-start(bf16[1,192,2048]{2,1,0:T(8,128)(2,1)} %param.13) | copy-start | bytes 2359300
  65.3 7.8 %copy-start.3 = (f32[128,8]{0,1:T(8,128)S(1)}, f32[128,8]{0,1:T(8,128)}, u32[]{:S(2)}) copy-start(f32[128,8]{0,1:T(8,128)} %param.10) | copy-start | bytes 12292
  65.3 43.3 %all-to-all-start = ((bf16[32,16,2048]{2,1,0:T(8,128)(2,1)}), bf16[32,16,2048]{2,1,0:T(8,128)(2,1)}, u32[]{:S(2)}, u32[]{:S(2)}) async-start(bf16[32,16,2048]{2,1,0:T(8,128)(2,1)} %broadcast_select_fusion), calls=%async_computation | async-start | bytes 4194304 | tf_op jit(solution)/shard_map/all_to_all | solution.py:97
  73.1 2.6 copy-start.2
  108.6 33.4 %all-to-all-start.2 = ((bf16[32,16,2048]{2,1,0:T(8,128)(2,1)}), bf16[32,16,2048]{2,1,0:T(8,128)(2,1)}, u32[]{:S(2)}, u32[]{:S(2)}) async-start(bf16[32,16,2048]{2,1,0:T(8,128)(2,1)} %fusion), calls=%async_computation.3 | async-start | bytes 4194304 | tf_op jit(solution)/shard_map/all_to_all | solution.py:107
  116.1 3.4 %copy-start.1 = (bf16[1,192,2048]{2,1,0:T(8,128)(2,1)S(1)}, bf16[1,192,2048]{2,1,0:T(8,128)(2,1)}, u32[]{:S(2)}) copy-start(bf16[1,192,2048]{2,1,0:T(8,128)(2,1)} %param.11) | copy-start | bytes 2359300
  146.8 33.6 %all-to-all-start.1 = ((bf16[32,16,2048]{2,1,0:T(8,128)(2,1)}), bf16[32,16,2048]{2,1,0:T(8,128)(2,1)}, u32[]{:S(2)}, u32[]{:S(2)}) async-start(bf16[32,16,2048]{2,1,0:T(8,128)(2,1)} %bitcast.67), calls=%async_computation.1 | async-start | bytes 4194304 | tf_op jit(solution)/shard_map/all_to_all | solution.py:100
  154.4 154.7 %reduce-scatter.3.cloned.1.call-start = ((), (), s32[]{:S(2)}) async-start(), calls=%async_computation.6 | async-start | bytes 1114112 | tf_op jit(solution)/shard_map/reduce_scatter | solution.py:134
  193.8 137.7 %reduce-scatter.5.cloned.1.call-start = ((), (), s32[]{:S(2)}) async-start(), calls=%async_computation.7 | async-start | bytes 1114112 | tf_op jit(solution)/shard_map/reduce_scatter | solution.py:135
Sparse Core Ops, SparseCore 0:
  193.9 66.0 reduce-scatter.2
  263.1 68.3 reduce-scatter.4
where the time goes:
time: 341 us; the launch traced here: 340 us
  blocking collectives  155 us (45%)
  waiting for transfers between devices  62.3 us (18%)
  other arithmetic  43.6 us (13%)
  matrix products  27.6 us (8%)
  starting transfers between devices  23.1 us (7%)
  between operations  14.3 us (4%)
  local copies, waits for them, and re-layouts  14.1 us (4%)
    psum x1, blocking collectives, per_device(): grad_gates = lax.psum(gate_part, 'expert')  54.9 us
    all_gather x1, blocking collectives, per_device(): lax.all_gather(tokens, 'expert', axis=1, tiled=True)  38.8 us
    all_to_all x1, blocking collectives, per_device(): lax.all_to_all(part_grad.reshape(dp_count, capacity, features), 'dp', spl...  32.4 us
    all_gather x1, blocking collectives, per_device(): lax.all_gather(cotangent, 'expert', axis=1, tiled=True)  28.7 us
    all_to_all x1, waiting for transfers between devices, per_device(): lax.all_to_all(expert_out.reshape(dp_count, capacity, features), 'dp', sp...  22 us
    reduce_scatter x1, waiting for transfers between devices, per_device(): lax.psum_scatter(grad_part, 'expert', scatter_dimension=1, tiled=True)  20.9 us
    all_to_all x1, waiting for transfers between devices, per_device(): lax.all_to_all(send_do, 'dp', split_axis=0, concat_axis=0, tiled=True)  19.4 us
    scatter-add x1, other arithmetic, per_device(): out_part = jnp.zeros((tok_count, width_now), jnp.float32).at[slot_token]....  9.44 us
  transfers between devices with their start and end apart: 5, of which 3 were waited for; matrix products, arithmetic and copies ran while one was open for 14% of the time, Pallas kernels for 0%

commit v1 on v0

--- a/solution.py
+++ b/solution.py
@@ -56,7 +56,9 @@
 def per_device(tokens, cotangent, expert_ids, gate_weights, w_gate, w_up, w_down):
     full_x, full_dy = (
         lax.all_gather(tokens, "expert", axis=1, tiled=True),
-        lax.all_gather(cotangent, "expert", axis=1, tiled=True),
+        jnp.concatenate(
+            lax.all_to_all(jnp.stack([cotangent] * lax.axis_size("expert")), "expert", 0, 0), axis=1
+        ),
     )
     dp_count = lax.axis_size("dp")
     column_count = lax.axis_size("expert")

time: 341 us -> 349 us (1.023)
  the two profiles are of different devices: /device:TPU:2 before, /device:TPU:10 now
where the time goes in v1:
time: 349 us; the launch traced here: 347 us
  blocking collectives  123 us (35%)
  waiting for transfers between devices  83.5 us (24%)
  other arithmetic  43.6 us (12%)
  starting transfers between devices  38.9 us (11%)
  matrix products  27.6 us (8%)
  local copies, waits for them, and re-layouts  16.9 us (5%)
  between operations  14.3 us (4%)
    psum x1, blocking collectives, per_device(): grad_gates = lax.psum(gate_part, 'expert')  54.1 us
    all_gather x1, blocking collectives, per_device(): lax.all_gather(tokens, 'expert', axis=1, tiled=True)  36 us
    all_to_all x1, blocking collectives, per_device(): lax.all_to_all(part_grad.reshape(dp_count, capacity, features), 'dp', spl...  32.6 us
    reduce_scatter x1, waiting for transfers between devices, per_device(): lax.psum_scatter(grad_part, 'expert', scatter_dimension=1, tiled=True)  24.6 us
    all_to_all x1, waiting for transfers between devices, per_device(): lax.all_to_all(expert_out.reshape(dp_count, capacity, features), 'dp', sp...  21.8 us
    all_to_all x1, waiting for transfers between devices, per_device(): lax.all_to_all(send_do, 'dp', split_axis=0, concat_axis=0, tiled=True)  19.2 us
    all_to_all x1, waiting for transfers between devices, per_device(): lax.all_to_all(send_x, 'dp', split_axis=0, concat_axis=0, tiled=True)  17.9 us
    all_to_all x1, starting transfers between devices, per_device(): lax.all_to_all(jnp.stack([cotangent] * lax.axis_size('expert')), 'expert'...  15.2 us
  transfers between devices with their start and end apart: 6, of which 4 were waited for; matrix products, arithmetic and copies ran while one was open for 19% of the time, Pallas kernels for 0%

profile of v1, /device:TPU:10, one launch (start us, length us, event | category | flops | bytes accessed | tf_op | source)
XLA Modules:
  0.0 347.5 jit_solution(8821853713130843004)
XLA Ops:
  8.9 15.2 %all-to-all-start.2 = ((bf16[16,128,128]{2,1,0:T(8,128)(2,1)}), bf16[16,128,128]{2,1,0:T(8,128)(2,1)}, u32[]{:S(2)}, u32[]{:S(2)}) async-start(bf16[16,128,128]{2,1,0:T(8,128)(2,1)} %stack.2), calls=%async_computation.3 | async-start | bytes 1048576 | tf_op jit(solution)/shard_map/all_to_all | solution.py:60
  25.4 9.0 %reduce-window.6 = s32[32,8,128]{2,1,0:T(8,128)S(1)} reduce-window(s32[32,8,128]{2,1,0:T(8,128)S(1)} %fusion.25, s32[]{:T(128)} %constant.66.clone.1), window={size=1x1x128 pad=0_0x0_0x127_0}, to_apply=%region_0.1 | reduce-window | flops 4161536 | bytes 262148 | tf_op jit(solution)/shard_map/reduce-window
  34.9 4.3 %scatter_custom_fusion = s32[512]{0:T(512)S(1)} fusion(s32[1024]{0:T(1024)S(1)} %bitcast.78, s32[1024]{0:T(1024)S(1)} %iota.11, s32[]{:T(128)} %constant.65.clone.1), kind=kCustom, calls=%fused_computation.92 | custom fusion | bytes 2052 | tf_op jit(solution)/shard_map/scatter | solution.py:85
  39.4 36.0 %all_gather.3 = bf16[128,2048]{1,0:T(8,128)(2,1)S(1)} all-gather(bf16[128,128]{1,0:T(8,128)(2,1)S(1)} %copy-done.2), channel_id=1, replica_groups=mesh['dp'=32,'expert'=16] {'expert'}, dimensions={1}, use_global_device_ids=true | all-gather | bytes 557056 | tf_op jit(solution)/shard_map/all_gather | solution.py:58
  79.5 7.7 %all-to-all-start = ((bf16[32,16,2048]{2,1,0:T(8,128)(2,1)}), bf16[32,16,2048]{2,1,0:T(8,128)(2,1)}, u32[]{:S(2)}, u32[]{:S(2)}) async-start(bf16[32,16,2048]{2,1,0:T(8,128)(2,1)} %broadcast_select_fusion), calls=%async_computation | async-start | bytes 4194304 | tf_op jit(solution)/shard_map/all_to_all | solution.py:99
  95.1 17.9 %all-to-all-done = bf16[32,16,2048]{2,1,0:T(8,128)(2,1)} async-done(((bf16[32,16,2048]{2,1,0:T(8,128)(2,1)}), bf16[32,16,2048]{2,1,0:T(8,128)(2,1)}, u32[]{:S(2)}, u32[]{:S(2)}) %all-to-all-start) | async-done | bytes 2097184 | tf_op jit(solution)/shard_map/all_to_all | solution.py:99
  113.0 7.8 %all-to-all-start.3 = ((bf16[32,16,2048]{2,1,0:T(8,128)(2,1)}), bf16[32,16,2048]{2,1,0:T(8,128)(2,1)}, u32[]{:S(2)}, u32[]{:S(2)}) async-start(bf16[32,16,2048]{2,1,0:T(8,128)(2,1)} %fusion), calls=%async_computation.4 | async-start | bytes 4194304 | tf_op jit(solution)/shard_map/all_to_all | solution.py:109
  120.8 3.4 fusion.11
  124.3 3.2 fusion.15
  127.4 19.2 %all-to-all-done.3 = bf16[32,16,2048]{2,1,0:T(8,128)(2,1)} async-done(((bf16[32,16,2048]{2,1,0:T(8,128)(2,1)}), bf16[32,16,2048]{2,1,0:T(8,128)(2,1)}, u32[]{:S(2)}, u32[]{:S(2)}) %all-to-all-start.3) | async-done | bytes 2097184 | tf_op jit(solution)/shard_map/all_to_all | solution.py:109
  151.4 7.8 %all-to-all-start.1 = ((bf16[32,16,2048]{2,1,0:T(8,128)(2,1)}), bf16[32,16,2048]{2,1,0:T(8,128)(2,1)}, u32[]{:S(2)}, u32[]{:S(2)}) async-start(bf16[32,16,2048]{2,1,0:T(8,128)(2,1)} %bitcast.73), calls=%async_computation.1 | async-start | bytes 4194304 | tf_op jit(solution)/shard_map/all_to_all | solution.py:102
  159.4 3.8 %fusion.13 = f32[512,2048]{1,0:T(8,128)} fusion(bf16[512,192]{0,1:T(8,128)(2,1)S(1)} %get-tuple-element.21, bf16[1,192,2048]{2,1,0:T(8,128)(2,1)} %param.11), kind=kOutput, calls=%fused_computation.29 | convolution fusion | flops 402653184 | bytes 5177344 | tf_op jit(solution)/shard_map/dot_general | solution.py:45
  163.3 21.8 %all-to-all-done.1 = bf16[32,16,2048]{2,1,0:T(8,128)(2,1)} async-done(((bf16[32,16,2048]{2,1,0:T(8,128)(2,1)}), bf16[32,16,2048]{2,1,0:T(8,128)(2,1)}, u32[]{:S(2)}, u32[]{:S(2)}) %all-to-all-start.1) | async-done | bytes 2097184 | tf_op jit(solution)/shard_map/all_to_all | solution.py:102
  185.0 3.9 %bitcast_multiply_fusion = f32[512,2048]{1,0:T(8,128)} fusion(f32[512]{0:T(512)S(1)} %broadcast_select_fusion.1, bf16[32,16,2048]{2,1,0:T(8,128)(2,1)} %all-to-all-done.1), kind=kLoop, calls=%fused_computation.13 | loop fusion | flops 2097152 | bytes 6293504 | tf_op jit(solution)/shard_map/mul | solution.py:125
  188.9 9.4 %scatter_custom_fusion.1 = f32[128,2048]{1,0:T(8,128)} fusion(s32[512]{0:T(512)S(1)} %get-tuple-element.24, f32[512,2048]{1,0:T(8,128)} %bitcast_multiply_fusion, f32[]{:T(128)} %constant.64.clone.1), kind=kCustom, calls=%fused_computation.35 | custom fusion | flops 1048576 | bytes 1049088 | tf_op jit(solution)/shard_map/scatter-add | solution.py:125
  198.5 3.2 add_convert_fusion
  201.6 32.6 %all_to_all.25 = bf16[32,16,2048]{2,1,0:T(8,128)(2,1)} all-to-all(bf16[32,16,2048]{2,1,0:T(8,128)(2,1)S(1)} %bitcast.72), channel_id=1, replica_groups=mesh['dp'=32,'expert'=16] {'dp'}, dimensions={0} | all-to-all | bytes 4194304 | tf_op jit(solution)/shard_map/all_to_all | solution.py:112
  234.2 9.1 %scatter_custom_fusion.2 = f32[128,2048]{1,0:T(8,128)} fusion(s32[512]{0:T(512)S(1)} %get-tuple-element.24, bf16[512,2048]{1,0:T(8,128)(2,1)} %bitcast.74, f32[]{:T(128)} %constant.64.clone.1), kind=kCustom, calls=%fused_computation.11 | custom fusion | flops 2097152 | bytes 3145732 | tf_op jit(solution)/shard_map/scatter-add | solution.py:127
  243.3 3.1 fusion.6
  246.4 3.1 fusion.5
  249.5 3.1 fusion.4
  254.8 3.5 scatter_custom_fusion.3
  258.4 54.1 %psum.7 = f32[128,8]{1,0:T(8,128)S(1)} all-reduce(f32[128,8]{1,0:T(8,128)S(1)} %reshape.247), channel_id=1, replica_groups=mesh['dp'=32,'expert'=16] {'expert'}, use_global_device_ids=true, to_apply=%region_10.11 | all-reduce | flops 1024 | bytes 8192 | tf_op jit(solution)/shard_map/psum | solution.py:139
  314.6 24.6 %reduce-scatter.5.cloned.1.call-done = f32[128,128]{1,0:T(8,128)} async-done(((f32[128,2048]{1,0:T(8,128)}), f32[128,128]{1,0:T(8,128)}) %reduce-scatter.5.cloned.1.call-update) | async-done | bytes 65552 | tf_op jit(solution)/shard_map/reduce_scatter | solution.py:137
  (56 shorter events, 26.4 us)
Async XLA Ops:
  7.2 139.5 %copy-start = (bf16[1,192,2048]{2,1,0:T(8,128)(2,1)S(1)}, bf16[1,192,2048]{2,1,0:T(8,128)(2,1)}, u32[]{:S(2)}) copy-start(bf16[1,192,2048]{2,1,0:T(8,128)(2,1)} %param.13) | copy-start | bytes 2359300
  7.2 32.2 %copy-start.2 = (bf16[128,128]{1,0:T(8,128)(2,1)S(1)}, bf16[128,128]{1,0:T(8,128)(2,1)}, u32[]{:S(2)}) copy-start(bf16[128,128]{1,0:T(8,128)(2,1)} %param.7) | copy-start | bytes 98308
  8.9 70.6 %all-to-all-start.2 = ((bf16[16,128,128]{2,1,0:T(8,128)(2,1)}), bf16[16,128,128]{2,1,0:T(8,128)(2,1)}, u32[]{:S(2)}, u32[]{:S(2)}) async-start(bf16[16,128,128]{2,1,0:T(8,128)(2,1)} %stack.2), calls=%async_computation.3 | async-start | bytes 1048576 | tf_op jit(solution)/shard_map/all_to_all | solution.py:60
  79.5 7.7 %copy-start.3 = (f32[128,8]{0,1:T(8,128)S(1)}, f32[128,8]{0,1:T(8,128)}, u32[]{:S(2)}) copy-start(f32[128,8]{0,1:T(8,128)} %param.10) | copy-start | bytes 12292
  79.5 33.5 %all-to-all-start = ((bf16[32,16,2048]{2,1,0:T(8,128)(2,1)}), bf16[32,16,2048]{2,1,0:T(8,128)(2,1)}, u32[]{:S(2)}, u32[]{:S(2)}) async-start(bf16[32,16,2048]{2,1,0:T(8,128)(2,1)} %broadcast_select_fusion), calls=%async_computation | async-start | bytes 4194304 | tf_op jit(solution)/shard_map/all_to_all | solution.py:99
  113.0 33.7 %all-to-all-start.3 = ((bf16[32,16,2048]{2,1,0:T(8,128)(2,1)}), bf16[32,16,2048]{2,1,0:T(8,128)(2,1)}, u32[]{:S(2)}, u32[]{:S(2)}) async-start(bf16[32,16,2048]{2,1,0:T(8,128)(2,1)} %fusion), calls=%async_computation.4 | async-start | bytes 4194304 | tf_op jit(solution)/shard_map/all_to_all | solution.py:109
  120.8 3.4 copy-start.1
  151.4 33.6 %all-to-all-start.1 = ((bf16[32,16,2048]{2,1,0:T(8,128)(2,1)}), bf16[32,16,2048]{2,1,0:T(8,128)(2,1)}, u32[]{:S(2)}, u32[]{:S(2)}) async-start(bf16[32,16,2048]{2,1,0:T(8,128)(2,1)} %bitcast.73), calls=%async_computation.1 | async-start | bytes 4194304 | tf_op jit(solution)/shard_map/all_to_all | solution.py:102
  159.2 153.9 %reduce-scatter.3.cloned.1.call-start = ((), (), s32[]{:S(2)}) async-start(), calls=%async_computation.7 | async-start | bytes 1114112 | tf_op jit(solution)/shard_map/reduce_scatter | solution.py:136
  198.4 140.8 %reduce-scatter.5.cloned.1.call-start = ((), (), s32[]{:S(2)}) async-start(), calls=%async_computation.8 | async-start | bytes 1114112 | tf_op jit(solution)/shard_map/reduce_scatter | solution.py:137
Sparse Core Ops, SparseCore 0:
  198.5 69.0 reduce-scatter.2
  270.7 68.4 reduce-scatter.4
